TPU v7x, 32 devices: a whole 2x2x4 slice. The times are simulated.
32 devices in a mesh: row: 4 (over y, x), col: 4 (over z), depth: 2 (over core).
Axes of the slice: x: 2, y: 2, z: 4, core: 2. Of those that a mesh axis runs over, the one named last changes fastest.
Arguments:
- blocks: float32 [24, 4, 6, 128, 128], P('row', 'col'), may hold values from -1.2 to 1.2
- columns: int32 [24, 4, 6], P('row', 'col'), may hold values from 0 to 23, as said below
- branch: int32 [24], P('row'), may hold values 0 or 1
Outputs:
- updated: float32 [24, 4, 6, 128, 128], P('row', 'col')
- traces: float32 [2], replicated
Inputs may be any that keep to these rules, and one draw needn't show every extreme that they name: Each block row names 6 distinct block columns in each column group g, all within g * 6 to (g + 1) * 6 - 1, and block row i names column i. `branch`: 1 selects the square for that block row, 0 selects 2 X minus the square.
All inputs are finite; a program needn't handle non-finite values.
Results may differ from a plain program's by a relative error of at most 0.0003.
Values sent between devices are 32-bit elements; how exact they have to be, the bound alone decides.
A program may use at most 64 MiB of HBM per device.

v0:
```python
import jax
import jax.numpy as jnp
from jax import lax
from jax.sharding import PartitionSpec as P

BS = 128
SPG = 6


EXACT = lax.Precision.HIGHEST


def shifted(value, axis, steps):
    count = lax.axis_size(axis)
    pairs = [(source, (source + steps) % count) for source in range(count)]
    return lax.ppermute(value, axis, pairs)


def cannon_sum(a_blocks, a_cols, out_cols, moving, moving_cols, offset, panel, passer):
    grid_rows = lax.axis_size("row")
    my_row = lax.axis_index("row")
    out_count = a_blocks.shape[0]
    slot_total = a_blocks.shape[1] * a_blocks.shape[2]
    a_flat = a_blocks.reshape(out_count, slot_total, BS, BS)
    a_cflat = a_cols.reshape(out_count, slot_total)
    tile_rows = moving.shape[0]
    start_sum = jnp.zeros((out_count, SPG, BS, BS), jnp.float32)

    def contribute(running, pieces, piece_cols, step_index):
        source = (my_row - step_index) % grid_rows
        wanted = source * panel + offset + jnp.arange(tile_rows, dtype=jnp.int32)
        hits = (a_cflat[:, :, None] == wanted[None, None, :]).astype(jnp.float32)
        stacked = jnp.einsum("nst,nsxy->tnxy", hits, a_flat, precision=EXACT)
        matches = (piece_cols[:, None, None, :] == out_cols[None, :, :, None]).astype(jnp.float32)

        def one_tile_row(total, items):
            left_side, right_side, pairing = items
            products = jnp.einsum("nxy,byz->nbxz", left_side, right_side, precision=EXACT)
            return (total + jnp.einsum("njb,nbxz->njxz", pairing, products, precision=EXACT), 0)

        running, unused = lax.scan(one_tile_row, running, (stacked, pieces, matches))
        return running

    def turn(step_index, carry):
        running, pieces, piece_cols = carry
        running = contribute(running, pieces, piece_cols, step_index)
        pieces, piece_cols = passer(pieces, piece_cols)
        return (running, pieces, piece_cols)

    running, pieces, piece_cols = lax.fori_loop(
        0, grid_rows - 1, turn, (start_sum, moving, moving_cols)
    )
    return contribute(running, pieces, piece_cols, grid_rows - 1)


def pass_whole(pieces, piece_cols):
    return shifted((pieces, piece_cols), "row", 1)


def on_device(blocks, columns, branch):
    panel = blocks.shape[0]
    layer_count = lax.axis_size("depth")
    layer = lax.axis_index("depth")
    my_row = lax.axis_index("row")
    rows_half = panel // layer_count
    first_row = layer * rows_half
    own_blocks = blocks[:, 0]
    own_cols = columns[:, 0]
    half_blocks = lax.dynamic_slice_in_dim(blocks, first_row, rows_half, 0)
    half_cols = lax.dynamic_slice_in_dim(columns, first_row, rows_half, 0)
    a_blocks, a_cols = (
        lax.all_gather(half_blocks, "col", axis=1, tiled=True),
        lax.all_gather(half_cols, "col", axis=1, tiled=True),
    )
    partial_sum = cannon_sum(
        a_blocks, a_cols, half_cols[:, 0], own_blocks, own_cols, 0, panel, pass_whole
    )
    product = lax.all_gather(partial_sum, "depth", axis=0, tiled=True)
    chooser = (branch == 1)[:, None, None, None]
    updated = jnp.where(chooser, product, 2.0 * own_blocks - product)
    row_ids = my_row * panel + jnp.arange(panel, dtype=jnp.int32)
    on_diag = (own_cols == row_ids[:, None]).astype(jnp.float32)
    old_term = jnp.sum(on_diag * jnp.trace(own_blocks, axis1=2, axis2=3))
    new_term = jnp.sum(on_diag * jnp.trace(updated, axis1=2, axis2=3))
    traces = lax.psum(jnp.stack([old_term, new_term]), ("row", "col"))
    return (updated[:, None], traces)


def solution(mesh):
    placed = (P("row", "col", None, None, None), P("row", "col", None), P("row"))
    return jax.shard_map(
        on_device,
        mesh=mesh,
        in_specs=placed,
        out_specs=(P("row", "col", None, None, None), P()),
        check_vma=False,
    )
```

profile of v0, /device:TPU:0, one launch (start us, length us, event | category | flops | bytes accessed | tf_op | source)
XLA Modules:
  0.0 425.1 jit_solution(3343656246658855847)
XLA Ops:
  7.2 2.5 constant_dynamic-slice_fusion.2
  9.9 13.6 %all_gather.9 = s32[3,4,6]{2,0,1:T(4,128)S(1)} all-gather(s32[3,1,6]{2,0,1:T(4,128)S(1)} %copy.50), channel_id=1, replica_groups=mesh['row'=4,'col'=4,'depth'=2] {'col'}, dimensions={1}, use_global_device_ids=true | all-gather | bytes 360 | tf_op jit(solution)/shard_map/all_gather | solution.py:73
  25.7 76.6 %all-gather.3.cloned.1.call-done = f32[3,4,6,128,128]{4,3,2,1,0:T(8,128)} async-done(((f32[3,1,6,128,128]{4,3,2,1,0:T(8,128)}), f32[3,4,6,128,128]{4,3,2,1,0:T(8,128)}) %all-gather.3.cloned.1.call-update) | async-done | bytes 4718608 | tf_op jit(solution)/shard_map/all_gather | solution.py:72
  102.3 7.3 %copy.26 = f32[3,24,128,128]{3,1,2,0:T(8,128)} copy(f32[3,24,128,128]{3,2,1,0:T(8,128)} %bitcast.113) | data formatting | bytes 9437184 | tf_op jit(solution)/shard_map/while | solution.py:50
  109.6 5.4 %convolution_bitcast_fusion.3 = f32[6,3,128,128]{3,0,2,1:T(8,128)} fusion(s32[3,24]{1,0:T(4,128)S(1)} %eq.163, s32[6]{0:T(128)S(1)} %iota_add_fusion.2, f32[3,24,128,128]{3,2,1,0:T(8,128)S(1)} %bitcast.114), kind=kOutput, calls=%fused_computation.28 | convolution fusion | flops 84935088 | bytes 5898552 | tf_op jit(solution)/shard_map/nst,nsxy->tnxy/dot_general | solution.py:33
  116.3 184.4 %while.59 = (s32[]{:T(128)}, f32[3,6,128,128]{3,1,2,0:T(8,128)}, f32[6,6,128,128]{2,3,1,0:T(8,128)}, s32[6,6]{1,0:T(8,128)S(1)}, s32[3,4,6]{2,1,0:T(4,128)}, /*i...) while((s32[]{:T(128)}, f32[3,6,128,128]{3,1,2,0:T(8,128)}, ...), condition=%wide.wide.region_3.4_spmd, body=%wide.wide.region_0.3_spmd.sunk | while | flops 559449792 | bytes 28524960 | solution.py:50
  117.8 3.3 copy.67
  122.7 5.1 %convolution_bitcast_fusion.9 = f32[6,3,128,128]{3,0,2,1:T(8,128)} fusion(f32[3,24,128,128]{3,1,2,0:T(8,128)} %get-tuple-element.582, s32[3,24]{1,0:T(4,128)S(1)} %get-tuple-element.584, s32[6]{0:T(128)S(1)} %iota_add_fusion.5), kind=kOutput, calls=%fused_computation.9.clone.clone.1 | convolution fusion | flops 84935088 | bytes 5898552 | tf_op jit(solution)/shard_map/while/body/eval_jaxpr/nst,nsxy->tnxy/dot_general | solution.py:33
  127.8 50.3 %while.60 = (s32[]{:T(128)}, f32[3,6,128,128]{3,1,2,0:T(8,128)}, f32[6,3,6,6]{3,2,1,0:T(8,128)S(1)}, f32[6,6,128,128]{2,3,1,0:T(8,128)}, f32[6,3,128,128]{3,0,2,1:T(8,128)}, /*index=5*/s32[]{:T(128)}) while((s32[]{:T(128)}, f32[3,6,128,128]{3,1,2,0:T(8,128)}, f32[6,3,6,6]{3,2,1,0:T(8,128)S(1)}, f32[6,6,128,128]{2,3,1,0:T(8,128)}, ...), condition=%wide.region_2.2_spmd, body=%wide.region_1.1_spmd.sunk | while | flops 474513408 | bytes 8466521 | solution.py:41
  129.4 2.1 convolution_bitcast_fusion.10
  132.1 4.1 convolution_add_fusion.5
  140.4 4.1 convolution_add_fusion.5
  148.8 4.1 convolution_add_fusion.5
  154.5 2.1 convolution_bitcast_fusion.10
  157.2 4.1 convolution_add_fusion.5
  165.6 4.1 convolution_add_fusion.5
  173.9 4.1 convolution_add_fusion.5
  179.6 3.3 copy.67
  183.5 5.1 %convolution_bitcast_fusion.9 = f32[6,3,128,128]{3,0,2,1:T(8,128)} fusion(f32[3,24,128,128]{3,1,2,0:T(8,128)} %get-tuple-element.582, s32[3,24]{1,0:T(4,128)S(1)} %get-tuple-element.584, s32[6]{0:T(128)S(1)} %iota_add_fusion.5), kind=kOutput, calls=%fused_computation.9.clone.clone.1 | convolution fusion | flops 84935088 | bytes 5898552 | tf_op jit(solution)/shard_map/while/body/eval_jaxpr/nst,nsxy->tnxy/dot_general | solution.py:33
  188.7 50.3 %while.60 = (s32[]{:T(128)}, f32[3,6,128,128]{3,1,2,0:T(8,128)}, f32[6,3,6,6]{3,2,1,0:T(8,128)S(1)}, f32[6,6,128,128]{2,3,1,0:T(8,128)}, f32[6,3,128,128]{3,0,2,1:T(8,128)}, /*index=5*/s32[]{:T(128)}) while((s32[]{:T(128)}, f32[3,6,128,128]{3,1,2,0:T(8,128)}, f32[6,3,6,6]{3,2,1,0:T(8,128)S(1)}, f32[6,6,128,128]{2,3,1,0:T(8,128)}, ...), condition=%wide.region_2.2_spmd, body=%wide.region_1.1_spmd.sunk | while | flops 474513408 | bytes 8466521 | solution.py:41
  192.9 4.1 convolution_add_fusion.5
  201.3 4.1 convolution_add_fusion.5
  209.7 4.1 convolution_add_fusion.5
  218.0 4.1 convolution_add_fusion.5
  223.8 2.1 convolution_bitcast_fusion.10
  226.4 4.1 convolution_add_fusion.5
  234.8 4.1 convolution_add_fusion.5
  240.4 3.3 copy.67
  245.3 5.1 %convolution_bitcast_fusion.9 = f32[6,3,128,128]{3,0,2,1:T(8,128)} fusion(f32[3,24,128,128]{3,1,2,0:T(8,128)} %get-tuple-element.582, s32[3,24]{1,0:T(4,128)S(1)} %get-tuple-element.584, s32[6]{0:T(128)S(1)} %iota_add_fusion.5), kind=kOutput, calls=%fused_computation.9.clone.clone.1 | convolution fusion | flops 84935088 | bytes 5898552 | tf_op jit(solution)/shard_map/while/body/eval_jaxpr/nst,nsxy->tnxy/dot_general | solution.py:33
  250.4 50.3 %while.60 = (s32[]{:T(128)}, f32[3,6,128,128]{3,1,2,0:T(8,128)}, f32[6,3,6,6]{3,2,1,0:T(8,128)S(1)}, f32[6,6,128,128]{2,3,1,0:T(8,128)}, f32[6,3,128,128]{3,0,2,1:T(8,128)}, /*index=5*/s32[]{:T(128)}) while((s32[]{:T(128)}, f32[3,6,128,128]{3,1,2,0:T(8,128)}, f32[6,3,6,6]{3,2,1,0:T(8,128)S(1)}, f32[6,6,128,128]{2,3,1,0:T(8,128)}, ...), condition=%wide.region_2.2_spmd, body=%wide.region_1.1_spmd.sunk | while | flops 474513408 | bytes 8466521 | solution.py:41
  252.0 2.1 convolution_bitcast_fusion.10
  254.7 4.1 convolution_add_fusion.5
  263.1 4.1 convolution_add_fusion.5
  271.5 4.1 convolution_add_fusion.5
  279.8 4.1 convolution_add_fusion.5
  288.2 4.1 convolution_add_fusion.5
  296.6 4.1 convolution_add_fusion.5
  300.8 57.6 %while.57 = (s32[]{:T(128)}, f32[3,6,128,128]{3,1,2,0:T(8,128)}, f32[6,3,6,6]{3,2,1,0:T(8,128)S(1)}, f32[6,6,128,128]{2,3,1,0:T(8,128)}, f32[6,3,128,128]{3,0,2,1:T(8,128)}, /*index=5*/s32[]{:T(128)}) while((s32[]{:T(128)}, f32[3,6,128,128]{3,1,2,0:T(8,128)}, f32[6,3,6,6]{3,2,1,0:T(8,128)S(1)}, f32[6,6,128,128]{2,3,1,0:T(8,128)}, ...), condition=%wide.region_5.6_spmd, body=%wide.region_4.5_spmd.sunk | while | flops 474513408 | bytes 18296976 | solution.py:41
  302.4 3.1 convolution_bitcast_fusion.8
  312.0 3.1 convolution_bitcast_fusion.8
  321.6 3.1 convolution_bitcast_fusion.8
  331.2 3.1 convolution_bitcast_fusion.8
  340.8 3.1 convolution_bitcast_fusion.8
  350.4 3.1 convolution_bitcast_fusion.8
  358.4 2.8 copy.30
  361.2 8.5 %all-gather.5.cloned.1.call-done = f32[6,6,128,128]{3,2,1,0:T(8,128)} async-done(((f32[3,6,128,128]{3,2,1,0:T(8,128)}), f32[6,6,128,128]{3,2,1,0:T(8,128)}) %all-gather.5.cloned.1.call-update) | async-done | bytes 2359312 | tf_op jit(solution)/shard_map/all_gather | solution.py:78
  369.8 3.7 select_reduce_fusion.1
  375.6 42.6 %psum.7 = f32[2]{0:T(128)} all-reduce(f32[2]{0:T(128)S(1)} %pad_maximum_fusion), channel_id=1, replica_groups=mesh['row'=4,'col'=4,'depth'=2] {'row','col'}, use_global_device_ids=true, to_apply=%region_10.11 | all-reduce | flops 2 | bytes 16 | tf_op jit(solution)/shard_map/psum | solution.py:85
  (144 shorter events, 120.9 us)
Async XLA Ops:
  7.2 95.1 %all-gather.3.cloned.1.call-start = ((), (), s32[]{:S(2)}) async-start(), calls=%async_computation | async-start | bytes 5898240 | tf_op jit(solution)/shard_map/all_gather | solution.py:72
  7.2 2.7 copy-start.6
  7.2 16.5 %copy-start.3 = (f32[6,1,6,128,128]{4,3,2,1,0:T(8,128)S(1)}, f32[6,1,6,128,128]{4,3,2,1,0:T(8,128)}, u32[]{:S(2)}) copy-start(f32[6,1,6,128,128]{4,3,2,1,0:T(8,128)} %param.9) | copy-start | bytes 7077892
  9.8 360.0 %all-gather.5.cloned.1.call-start = ((), (), s32[]{:S(2)}) async-start(), calls=%async_computation.1 | async-start | bytes 3538944 | tf_op jit(solution)/shard_map/all_gather | solution.py:78
  23.6 2.1 copy-start.5
  102.3 7.3 %copy-start.2 = (f32[3,4,6,128,128]{4,3,2,1,0:T(8,128)S(1)}, f32[3,4,6,128,128]{4,3,2,1,0:T(8,128)}, u32[]{:S(2)}) copy-start(f32[3,4,6,128,128]{4,3,2,1,0:T(8,128)} %all-gather.3.cloned.1.call-done) | copy-start | bytes 14155780
  116.3 61.7 %collective-permute-start.1 = (s32[6,6]{1,0:T(8,128)S(1)}, s32[6,6]{1,0:T(8,128)S(1)}, u32[]{:S(2)}, u32[]{:S(2)}) collective-permute-start(s32[6,6]{1,0:T(8,128)S(1)} %copy.68), channel_id=1, source_target_pairs={{0,8},{8,16},{16,24},{24,0},{1,9},{9,17},{17,25},{25,1},{2,10},{10... | collective-permute-start | bytes 440 | tf_op jit(solution)/shard_map/while/body/eval_jaxpr/ppermute | solution.py:16
  121.1 56.9 %collective-permute-start = (f32[6,6,128,128]{2,3,1,0:T(8,128)}, f32[6,6,128,128]{2,3,1,0:T(8,128)}, u32[]{:S(2)}, u32[]{:S(2)}) collective-permute-start(f32[6,6,128,128]{2,3,1,0:T(8,128)} %copy.67), channel_id=1, source_target_pairs={{0,8},{8,16},{16,24},{24,0},{1,9},{9,17},{17,25},{25,1},{2,10},{10... | collective-permute-start | bytes 7077896 | tf_op jit(solution)/shard_map/while/body/eval_jaxpr/ppermute | solution.py:16
  178.1 60.9 %collective-permute-start.1 = (s32[6,6]{1,0:T(8,128)S(1)}, s32[6,6]{1,0:T(8,128)S(1)}, u32[]{:S(2)}, u32[]{:S(2)}) collective-permute-start(s32[6,6]{1,0:T(8,128)S(1)} %copy.68), channel_id=1, source_target_pairs={{0,8},{8,16},{16,24},{24,0},{1,9},{9,17},{17,25},{25,1},{2,10},{10... | collective-permute-start | bytes 440 | tf_op jit(solution)/shard_map/while/body/eval_jaxpr/ppermute | solution.py:16
  182.9 56.0 %collective-permute-start = (f32[6,6,128,128]{2,3,1,0:T(8,128)}, f32[6,6,128,128]{2,3,1,0:T(8,128)}, u32[]{:S(2)}, u32[]{:S(2)}) collective-permute-start(f32[6,6,128,128]{2,3,1,0:T(8,128)} %copy.67), channel_id=1, source_target_pairs={{0,8},{8,16},{16,24},{24,0},{1,9},{9,17},{17,25},{25,1},{2,10},{10... | collective-permute-start | bytes 7077896 | tf_op jit(solution)/shard_map/while/body/eval_jaxpr/ppermute | solution.py:16
  238.9 61.8 %collective-permute-start.1 = (s32[6,6]{1,0:T(8,128)S(1)}, s32[6,6]{1,0:T(8,128)S(1)}, u32[]{:S(2)}, u32[]{:S(2)}) collective-permute-start(s32[6,6]{1,0:T(8,128)S(1)} %copy.68), channel_id=1, source_target_pairs={{0,8},{8,16},{16,24},{24,0},{1,9},{9,17},{17,25},{25,1},{2,10},{10... | collective-permute-start | bytes 440 | tf_op jit(solution)/shard_map/while/body/eval_jaxpr/ppermute | solution.py:16
  243.8 56.9 %collective-permute-start = (f32[6,6,128,128]{2,3,1,0:T(8,128)}, f32[6,6,128,128]{2,3,1,0:T(8,128)}, u32[]{:S(2)}, u32[]{:S(2)}) collective-permute-start(f32[6,6,128,128]{2,3,1,0:T(8,128)} %copy.67), channel_id=1, source_target_pairs={{0,8},{8,16},{16,24},{24,0},{1,9},{9,17},{17,25},{25,1},{2,10},{10... | collective-permute-start | bytes 7077896 | tf_op jit(solution)/shard_map/while/body/eval_jaxpr/ppermute | solution.py:16
  305.5 1.9 copy-start
  309.1 1.2 copy-start.1
  315.1 1.9 copy-start
  318.7 1.2 copy-start.1
  324.7 1.9 copy-start
  328.3 1.2 copy-start.1
  334.3 1.9 copy-start
  337.9 1.2 copy-start.1
  343.9 1.9 copy-start
  347.5 1.2 copy-start.1
  353.5 1.9 copy-start
  357.1 1.2 copy-start.1
  358.4 2.8 copy-start.7
  358.4 11.4 %copy-start.4 = (f32[6,1,6,128,128]{4,3,2,1,0:T(8,128)S(1)}, f32[6,1,6,128,128]{4,3,2,1,0:T(8,128)}, u32[]{:S(2)}) copy-start(f32[6,1,6,128,128]{4,3,2,1,0:T(8,128)} %param.9) | copy-start | bytes 7077892
Sparse Core Ops, SparseCore 0:
  10.1 92.0 all-gather.2
  361.3 8.4 all-gather.4
where the time goes:
time: 428 us; the launch traced here: 425 us
  matrix products  161 us (38%)
  local copies, waits for them, and re-layouts  93.4 us (22%)
  waiting for transfers between devices  85.2 us (20%)
  blocking collectives  56.3 us (13%)
  between operations  14.2 us (3%)
  starting transfers between devices  8.07 us (2%)
  other arithmetic  6.19 us (1%)
    dot_general x24, matrix products, one_tile_row(): jnp.einsum('njb,nbxz->njxz', pairing, products, precision=EXACT)  84.3 us
    all_gather x1, waiting for transfers between devices, on_device(): lax.all_gather(half_blocks, 'col', axis=1, tiled=True)  76.6 us
    dot_general x24, matrix products, one_tile_row(): jnp.einsum('nxy,byz->nbxz', left_side, right_side, precision=EXACT)  56.3 us
    psum x1, blocking collectives, on_device(): traces = lax.psum(jnp.stack([old_term, new_term]), ('row', 'col'))  42.6 us
    dynamic_slice x24, local copies, waits for them, and re-layouts, contribute(): lax.scan(one_tile_row, running, (stacked, pieces, matches))  38.2 us
    transpose x24, local copies, waits for them, and re-layouts, one_tile_row(): jnp.einsum('nxy,byz->nbxz', left_side, right_side, precision=EXACT)  21.6 us
    dot_general x4, matrix products, contribute(): stacked = jnp.einsum('nst,nsxy->tnxy', hits, a_flat, precision=EXACT)  20.8 us
    all_gather x1, blocking collectives, on_device(): lax.all_gather(half_cols, 'col', axis=1, tiled=True)  13.6 us
  transfers between devices with their start and end apart: 8, of which 2 were waited for; matrix products, arithmetic and copies ran while one was open for 42% of the time, Pallas kernels for 0%

commit v1 on v0

--- a/solution.py
+++ b/solution.py
@@ -1,6 +1,10 @@
+import functools
+
 import jax
 import jax.numpy as jnp
 from jax import lax
+from jax.experimental import pallas as pl
+from jax.experimental.pallas import tpu as pltpu
 from jax.sharding import PartitionSpec as P
 
 BS = 128
@@ -86,10 +90,328 @@
     return (updated[:, None], traces)
 
 
+MESH = pl.DeviceIdType.MESH
+CHUNKS = 2
+
+
+def place_kernel(cols_ref, blocks_ref, out_ref):
+    row = pl.program_id(0)
+    for slot in range(blocks_ref.shape[2]):
+        at = lax.rem(cols_ref[row, slot], blocks_ref.shape[2])
+        out_ref[:, pl.ds(pl.multiple_of(at * BS, BS), BS)] = blocks_ref[0, 0, slot]
+
+
+def place(blocks, cols):
+    panel, _, slots = blocks.shape[:3]
+    return pl.pallas_call(
+        place_kernel,
+        grid_spec=pltpu.PrefetchScalarGridSpec(
+            num_scalar_prefetch=1,
+            grid=(panel,),
+            in_specs=[pl.BlockSpec((1, 1, slots, BS, BS), lambda i, c: (i, 0, 0, 0, 0))],
+            out_specs=pl.BlockSpec((BS, slots * BS), lambda i, c: (i, 0)),
+        ),
+        out_shape=jax.ShapeDtypeStruct((panel * BS, slots * BS), jnp.float32),
+    )(cols, blocks)
+
+
+def halves(value):
+    high = value.astype(jnp.bfloat16)
+    return high, (value - high.astype(jnp.float32)).astype(jnp.bfloat16)
+
+
+def square_kernel(
+    groups, cols_ref, branch_ref, tile, blocks_ref, out_ref, trace_ref,
+    left, right, right_hi, right_lo, total, parts,
+    z_send, z_recv, p_send, p_recv, sz_send, sz_recv, sp_send, sp_recv, t_send, t_recv,
+):
+    row, col, depth = lax.axis_index("row"), lax.axis_index("col"), lax.axis_index("depth")
+    panel, slots = blocks_ref.shape[0], blocks_ref.shape[2]
+    rows = tile.shape[0]
+    half = rows // 2
+    step = half // CHUNKS
+    sibling = (row, col, 1 - depth)
+    across = (row + 1 - 2 * (row % 2), (row + 2) % 4)
+    corner = across[1] + 1 - 2 * (row % 2)
+
+    barrier = pltpu.get_barrier_semaphore()
+
+    def greet(peer, carry):
+        @pl.when(peer != row * groups + col)
+        def _():
+            pl.semaphore_signal(
+                barrier, inc=1, device_id=(peer // groups, peer % groups, depth), device_id_type=MESH
+            )
+        return carry
+
+    pl.semaphore_signal(barrier, inc=1, device_id=sibling, device_id_type=MESH)
+    lax.fori_loop(0, 4 * groups, greet, 0)
+    pl.semaphore_wait(barrier, 4 * groups)
+
+    def span(core, chunk):
+        return pl.ds(pl.multiple_of(core * half + chunk * step, step), step)
+
+    def copy(src, dst, send, recv, target):
+        return pltpu.make_async_remote_copy(
+            src_ref=src, dst_ref=dst, send_sem=send, recv_sem=recv, device_id=target, device_id_type=MESH
+        )
+
+    def z_source(side, hop):
+        return col - hop if side == 0 else col + hop
+
+    def z_has(side, hop):
+        return col >= hop if side == 0 else col + hop < groups
+
+    def z_goes(side, hop):
+        ahead = col + 1 < groups if side == 0 else col >= 1
+        if hop == 1:
+            return ahead
+        return jnp.logical_and(ahead, z_has(side, hop - 1))
+
+    def z_copy(side, hop, chunk):
+        source = z_source(side, hop - 1)
+        at = span(depth, chunk)
+        src = tile.at[at] if hop == 1 else left.at[source, at]
+        target = (row, jnp.clip(col + 1, 0, groups - 1) if side == 0 else jnp.clip(col - 1, 0, groups - 1), depth)
+        return copy(src, left.at[source, at], z_send.at[side, hop - 1, chunk], z_recv.at[side, hop - 1, chunk], target)
+
+    def z_arrival(side, hop, chunk):
+        place_at = left.at[z_source(side, hop), span(depth, chunk)]
+        return copy(place_at, place_at, z_send.at[side, hop - 1, chunk], z_recv.at[side, hop - 1, chunk], sibling)
+
+    def z_share(side, hop, chunk, core):
+        place_at = left.at[z_source(side, hop), span(core, chunk)]
+        return copy(place_at, place_at, sz_send.at[side, hop - 1, chunk], sz_recv.at[side, hop - 1, chunk], sibling)
+
+    def z_take(hop, chunk):
+        for side in range(2):
+            @pl.when(z_has(side, hop))
+            def _(side=side):
+                z_arrival(side, hop, chunk).wait_recv()
+                if hop + 1 < groups:
+                    @pl.when(z_goes(side, hop + 1))
+                    def _():
+                        z_copy(side, hop + 1, chunk).start()
+                z_share(side, hop, chunk, depth).start()
+
+    def p_copy(axis, piece):
+        target = (across[axis], col, depth)
+        if piece < CHUNKS:
+            at = span(depth, piece)
+            src, dst = tile.at[at], right.at[row, at]
+        else:
+            at = span(depth, axis)
+            src = dst = right.at[across[1 - axis], at]
+        return copy(src, dst, p_send.at[axis, piece], p_recv.at[axis, piece], target)
+
+    def p_place(axis, piece, core):
+        if piece < CHUNKS:
+            return right.at[across[axis], span(core, piece)]
+        return right.at[corner, span(core, axis)]
+
+    def p_arrival(axis, piece):
+        place_at = p_place(axis, piece, depth)
+        return copy(place_at, place_at, p_send.at[axis, piece], p_recv.at[axis, piece], sibling)
+
+    def p_share(axis, piece, core):
+        place_at = p_place(axis, piece, core)
+        return copy(place_at, place_at, sp_send.at[axis, piece], sp_recv.at[axis, piece], sibling)
+
+    for chunk in range(CHUNKS):
+        for side in range(2):
+            @pl.when(z_goes(side, 1))
+            def _(side=side, chunk=chunk):
+                z_copy(side, 1, chunk).start()
+        for axis in range(2):
+            p_copy(axis, chunk).start()
+
+    block_rows = rows // 4
+
+    def split_right(source, index):
+        def some(part, carry):
+            at = pl.ds(pl.multiple_of(part * block_rows, block_rows), block_rows)
+            high, low = halves(source[at])
+            right_hi[index, at] = high
+            right_lo[index, at] = low
+            return carry
+        lax.fori_loop(0, 4, some, 0)
+
+    def multiply(source, index, at, first=False):
+        high, low = halves(source[at])
+        dot = functools.partial(jnp.dot, preferred_element_type=jnp.float32)
+        product = (dot(high, right_lo[index]) + dot(low, right_hi[index])) + dot(high, right_hi[index])
+        for block in range(slots):
+            piece = product[:, block * BS:(block + 1) * BS]
+            total[block, at] = piece if first else total[block, at] + piece
+
+    def multiply_all(source, index, first=False):
+        def some(part, carry):
+            multiply(source, index, pl.ds(pl.multiple_of(part * block_rows, block_rows), block_rows), first)
+            return carry
+        lax.fori_loop(0, 4, some, 0)
+
+    split_right(tile, row)
+
+    for chunk in range(CHUNKS):
+        z_take(1, chunk)
+        for axis in range(2):
+            p_arrival(axis, chunk).wait_recv()
+            if chunk == 1 - axis:
+                p_copy(1 - axis, CHUNKS).start()
+            p_share(axis, chunk, depth).start()
+    for axis in range(2):
+        for chunk in range(CHUNKS):
+            p_share(axis, chunk, 1 - depth).wait_recv()
+        split_right(right.at[across[axis]], across[axis])
+    for axis in range(2):
+        p_arrival(axis, CHUNKS).wait_recv()
+        p_share(axis, CHUNKS, depth).start()
+    for axis in range(2):
+        p_share(axis, CHUNKS, 1 - depth).wait_recv()
+    split_right(right.at[corner], corner)
+    multiply_all(tile, col, True)
+
+    def z_multiply(hop, chunk):
+        for side in range(2):
+            @pl.when(z_has(side, hop))
+            def _(side=side):
+                source = z_source(side, hop)
+                multiply(left.at[source], source, span(depth, chunk))
+                z_share(side, hop, chunk, 1 - depth).wait_recv()
+                multiply(left.at[source], source, span(1 - depth, chunk))
+
+    for hop in range(2, groups):
+        for chunk in range(CHUNKS):
+            z_take(hop, chunk)
+            if (hop, chunk) == (2, 0):
+                for early in range(CHUNKS):
+                    z_multiply(1, early)
+            z_multiply(hop, chunk)
+
+    eye = lax.broadcasted_iota(jnp.int32, (BS, BS), 0) == lax.broadcasted_iota(jnp.int32, (BS, BS), 1)
+    spot = lax.broadcasted_iota(jnp.int32, parts.shape[1:], 1)
+
+    @pl.when(row == col)
+    def _():
+        old_sum = jnp.zeros((BS, BS), jnp.float32)
+        new_sum = jnp.zeros((BS, BS), jnp.float32)
+        for block in range(panel):
+            at = pl.ds(block * BS, BS)
+            old = tile[at, at]
+            square = total[block, at]
+            new = jnp.where(branch_ref[block] == 1, square, 2.0 * old - square)
+            old_sum += jnp.where(eye, old, 0.0)
+            new_sum += jnp.where(eye, new, 0.0)
+        old_all, new_all = jnp.sum(old_sum), jnp.sum(new_sum)
+        parts[row] = jnp.where(spot == 0, old_all, jnp.where(spot == 1, new_all, 0.0))
+
+    def finish(block, carry):
+        at = pl.ds(pl.multiple_of(block * BS, BS), BS)
+        taken = branch_ref[block] == 1
+        for slot in range(slots):
+            square = total[lax.rem(cols_ref[block, slot], slots), at]
+            out_ref[block, 0, slot] = jnp.where(taken, square, 2.0 * blocks_ref[block, 0, slot] - square)
+        return carry
+
+    lax.fori_loop(0, panel, finish, 0)
+
+    def t_copy(peer):
+        return copy(parts.at[row], parts.at[row], t_send.at[peer], t_recv.at[row], (peer // groups, peer % groups, depth))
+
+    def to_peers(act):
+        def one(peer, carry):
+            @pl.when(peer != row * groups + col)
+            def _():
+                act(t_copy(peer))
+            return carry
+        lax.fori_loop(0, 4 * groups, one, 0)
+
+    @pl.when(row == col)
+    def _():
+        to_peers(lambda c: c.start())
+
+    for source in range(groups):
+        @pl.when(jnp.logical_or(row != source, col != source))
+        def _(source=source):
+            copy(parts.at[source], parts.at[source], t_send.at[source], t_recv.at[source], sibling).wait_recv()
+    sum_all = parts[0]
+    for source in range(1, groups):
+        sum_all = sum_all + parts[source]
+    trace_ref[...] = sum_all
+
+    @pl.when(row == col)
+    def _():
+        to_peers(lambda c: c.wait_send())
+
+    for axis in range(2):
+        for piece in range(CHUNKS + 1):
+            p_copy(axis, piece).wait_send()
+            p_share(axis, piece, depth).wait_send()
+    for side in range(2):
+        for hop in range(1, groups):
+            for chunk in range(CHUNKS):
+                @pl.when(z_goes(side, hop))
+                def _(side=side, hop=hop, chunk=chunk):
+                    z_copy(side, hop, chunk).wait_send()
+
+                @pl.when(z_has(side, hop))
+                def _(side=side, hop=hop, chunk=chunk):
+                    z_share(side, hop, chunk, depth).wait_send()
+
+
+def full_rows(groups, blocks, columns, branch):
+    panel, _, slots = blocks.shape[:3]
+    cols = columns[:, 0]
+    tile = place(blocks, cols)
+    size = panel * BS
+    sems = pltpu.SemaphoreType.DMA
+    vmem = pl.BlockSpec(memory_space=pltpu.VMEM)
+    smem = pl.BlockSpec(memory_space=pltpu.SMEM)
+    updated, traces = pl.pallas_call(
+        functools.partial(square_kernel, groups),
+        out_shape=(
+            jax.ShapeDtypeStruct(blocks.shape, jnp.float32),
+            jax.ShapeDtypeStruct((8, BS), jnp.float32),
+        ),
+        in_specs=[smem, smem, vmem, vmem],
+        out_specs=(vmem, vmem),
+        scratch_shapes=[
+            pltpu.VMEM((groups, size, size), jnp.float32),
+            pltpu.VMEM((groups, size, size), jnp.float32),
+            pltpu.VMEM((groups, size, size), jnp.bfloat16),
+            pltpu.VMEM((groups, size, size), jnp.bfloat16),
+            pltpu.VMEM((slots, size, BS), jnp.float32),
+            pltpu.VMEM((groups, 8, BS), jnp.float32),
+            sems((2, groups - 1, CHUNKS)),
+            sems((2, groups - 1, CHUNKS)),
+            sems((2, CHUNKS + 1)),
+            sems((2, CHUNKS + 1)),
+            sems((2, groups - 1, CHUNKS)),
+            sems((2, groups - 1, CHUNKS)),
+            sems((2, CHUNKS + 1)),
+            sems((2, CHUNKS + 1)),
+            sems((4 * groups,)),
+            sems((groups,)),
+        ],
+        compiler_params=pltpu.CompilerParams(
+            collective_id=0, has_side_effects=True, vmem_limit_bytes=60 * 2**20
+        ),
+    )(cols, branch, tile, blocks)
+    return updated, traces[0, :2]
+
+
 def solution(mesh):
     placed = (P("row", "col", None, None, None), P("row", "col", None), P("row"))
+    grid = mesh.shape["row"], mesh.shape["col"], mesh.shape["depth"]
+
+    def per_device(blocks, columns, branch):
+        panel, _, slots = blocks.shape[:3]
+        if grid[0] == 4 and grid[1] == 4 and grid[2] == 2 and panel == slots:
+            return full_rows(grid[1], blocks, columns, branch)
+        return on_device(blocks, columns, branch)
+
     return jax.shard_map(
-        on_device,
+        per_device,
         mesh=mesh,
         in_specs=placed,
         out_specs=(P("row", "col", None, None, None), P()),

time: 428 us -> 108 us (0.25)
  matrix products: 161 us -> 0 us
  Pallas kernels: 0 us -> 101 us
  local copies, waits for them, and re-layouts: 93.4 us -> 5.78 us
  waiting for transfers between devices: 85.2 us -> 0 us
  blocking collectives: 56.3 us -> 0 us
  between operations: 14.2 us -> 0.64 us
  starting transfers between devices: 8.07 us -> 0 us
  other arithmetic: 6.19 us -> 0 us
    dot_general x52 -> x0, matrix products: 161 us -> none  [the longest x24 84.3 us: one_tile_row(): jnp.einsum('njb,nbxz->njxz', pairing, products, precision=EXACT)]
    pallas_call x0 -> x2, Pallas kernels: none -> 101 us  [the longest x1 95.8 us: full_rows(): pl.pallas_call(functools.partial(square_kernel, groups), out_shape=(jax.S...]
    all_gather x2 -> x0, waiting for transfers between devices: 85.1 us -> none  [the longest x1 76.6 us: on_device(): lax.all_gather(half_blocks, 'col', axis=1, tiled=True)]
    psum x1 -> x0, blocking collectives: 42.6 us -> none  [on_device(): traces = lax.psum(jnp.stack([old_term, new_term]), ('row', 'col'))]
    dynamic_slice x26 -> x0, local copies, waits for them, and re-layouts: 40.8 us -> none  [the longest x24 38.2 us: contribute(): lax.scan(one_tile_row, running, (stacked, pieces, matches))]
    transpose x24 -> x0, local copies, waits for them, and re-layouts: 21.6 us -> none  [one_tile_row(): jnp.einsum('nxy,byz->nbxz', left_side, right_side, precision=EXACT)]
    while x28 -> x0, local copies, waits for them, and re-layouts: 19.5 us -> none  [the longest x3 9.3 us: cannon_sum(): lax.fori_loop(0, grid_rows - 1, turn, (start_sum, moving, moving_cols))]
    all_gather x1 -> x0, blocking collectives: 13.6 us -> none  [on_device(): lax.all_gather(half_cols, 'col', axis=1, tiled=True)]
  transfers between devices with their start and end apart: 8 -> 0, of which waited for: 2 -> 0; matrix products, arithmetic and copies ran while one was open for 42% -> 0% of each run, Pallas kernels for 0% -> 0%
where the time goes in v1:
time: 108 us
  Pallas kernels  101 us (94%)
  local copies, waits for them, and re-layouts  5.78 us (5%)
    pallas_call x1, Pallas kernels, full_rows(): pl.pallas_call(functools.partial(square_kernel, groups), out_shape=(jax.S...  95.8 us
    pallas_call x1, Pallas kernels, place(): pl.pallas_call(place_kernel, grid_spec=pltpu.PrefetchScalarGridSpec(num_s...  5.65 us
    unnamed x2, local copies, waits for them, and re-layouts  4.59 us

profile of v1, /device:TPU:0, one launch (start us, length us, event | category | flops | bytes accessed | tf_op | source)
XLA Modules:
  0.0 107.8 jit_solution(15127995815069014151)
XLA Ops:
  0.6 1.3 %copy.7 = s32[6,1,6]{2,0,1:T(8,128)} copy(s32[6,1,6]{2,1,0:T(1,128)} %param.4) | data formatting | bytes 288
  1.9 5.7 %shard_map.50.tile = f32[768,768]{1,0:T(8,128)} custom-call(s32[6,6]{1,0:T(8,128)} %bitcast.5, f32[6,1,6,128,128]{4,3,2,1,0:T(8,128)} %blocks_ref.3), custom_call_target="tpu_custom_call" | custom-call | tf_op jit(solution)/shard_map/pallas_call | solution.py:106
  7.6 95.8 %shard_map.51 = (f32[6,1,6,128,128]{4,3,2,1,0:T(8,128)}, f32[8,128]{1,0:T(8,128)}) custom-call(s32[6,6]{1,0:T(8,128)} %bitcast.6, s32[6]{0:T(128)} %branch_ref.1, f32[768,768]{1,0:T(8,128)} %shard_map.50.tile, f32[6,1,6,128,128]{4,3,2,1,0:T(8,128)} %blocks_ref.3), custom_call_target="tpu_custom_call" | custom-call | tf_op jit(solution)/shard_map/pallas_call | solution.py:370
  103.3 1.2 %slice_bitcast_fusion = f32[2]{0:T(128)} fusion(f32[8,128]{1,0:T(8,128)} %get-tuple-element.5), kind=kLoop, calls=%fused_computation.1 | loop fusion | bytes 16 | tf_op jit(solution)/shard_map/squeeze | solution.py:400
  104.5 3.3 %copy.9 = f32[6,1,6,128,128]{4,3,2,1,0:T(8,128)} copy(f32[6,1,6,128,128]{4,3,2,1,0:T(8,128)} %get-tuple-element.8) | data formatting | bytes 4718592

commit v2 on v1

--- a/solution.py
+++ b/solution.py
@@ -94,39 +94,18 @@
 CHUNKS = 2
 
 
-def place_kernel(cols_ref, blocks_ref, out_ref):
-    row = pl.program_id(0)
-    for slot in range(blocks_ref.shape[2]):
-        at = lax.rem(cols_ref[row, slot], blocks_ref.shape[2])
-        out_ref[:, pl.ds(pl.multiple_of(at * BS, BS), BS)] = blocks_ref[0, 0, slot]
-
-
-def place(blocks, cols):
-    panel, _, slots = blocks.shape[:3]
-    return pl.pallas_call(
-        place_kernel,
-        grid_spec=pltpu.PrefetchScalarGridSpec(
-            num_scalar_prefetch=1,
-            grid=(panel,),
-            in_specs=[pl.BlockSpec((1, 1, slots, BS, BS), lambda i, c: (i, 0, 0, 0, 0))],
-            out_specs=pl.BlockSpec((BS, slots * BS), lambda i, c: (i, 0)),
-        ),
-        out_shape=jax.ShapeDtypeStruct((panel * BS, slots * BS), jnp.float32),
-    )(cols, blocks)
-
-
 def halves(value):
     high = value.astype(jnp.bfloat16)
     return high, (value - high.astype(jnp.float32)).astype(jnp.bfloat16)
 
 
 def square_kernel(
-    groups, cols_ref, branch_ref, tile, blocks_ref, out_ref, trace_ref,
-    left, right, right_hi, right_lo, total, parts,
+    groups, cols_ref, branch_ref, blocks_hbm, out_ref, trace_ref,
+    blocks_ref, tile, in_sem, left, right, right_hi, right_lo, total, parts,
     z_send, z_recv, p_send, p_recv, sz_send, sz_recv, sp_send, sp_recv, t_send, t_recv,
 ):
     row, col, depth = lax.axis_index("row"), lax.axis_index("col"), lax.axis_index("depth")
-    panel, slots = blocks_ref.shape[0], blocks_ref.shape[2]
+    panel, slots = blocks_ref.shape[:2]
     rows = tile.shape[0]
     half = rows // 2
     step = half // CHUNKS
@@ -146,6 +125,27 @@
 
     pl.semaphore_signal(barrier, inc=1, device_id=sibling, device_id_type=MESH)
     lax.fori_loop(0, 4 * groups, greet, 0)
+
+    per_half = panel // 2
+
+    def ordered(block):
+        at = pl.ds(pl.multiple_of(block * BS, BS), BS)
+        for target_slot in range(slots):
+            source = 0
+            for slot in range(1, slots):
+                source = jnp.where(lax.rem(cols_ref[block, 0, slot], slots) == target_slot, slot, source)
+            tile[at, target_slot * BS:(target_slot + 1) * BS] = blocks_ref[block, source]
+
+    def incoming(turn):
+        block = lax.rem(depth * per_half + turn, panel)
+        return block, pltpu.make_async_copy(blocks_hbm.at[block, 0], blocks_ref.at[block], in_sem.at[turn])
+
+    for turn in range(panel):
+        incoming(turn)[1].start()
+    for turn in range(panel):
+        incoming(turn)[1].wait()
+    for turn in range(panel):
+        ordered(incoming(turn)[0])
     pl.semaphore_wait(barrier, 4 * groups)
 
     def span(core, chunk):
@@ -309,11 +309,9 @@
         at = pl.ds(pl.multiple_of(block * BS, BS), BS)
         taken = branch_ref[block] == 1
         for slot in range(slots):
-            square = total[lax.rem(cols_ref[block, slot], slots), at]
-            out_ref[block, 0, slot] = jnp.where(taken, square, 2.0 * blocks_ref[block, 0, slot] - square)
+            square = total[lax.rem(cols_ref[block, 0, slot], slots), at]
+            out_ref[block, 0, slot] = jnp.where(taken, square, 2.0 * blocks_ref[block, slot] - square)
         return carry
-
-    lax.fori_loop(0, panel, finish, 0)
 
     def t_copy(peer):
         return copy(parts.at[row], parts.at[row], t_send.at[peer], t_recv.at[row], (peer // groups, peer % groups, depth))
@@ -325,6 +323,8 @@
                 act(t_copy(peer))
             return carry
         lax.fori_loop(0, 4 * groups, one, 0)
+
+    lax.fori_loop(0, panel, finish, 0)
 
     @pl.when(row == col)
     def _():
@@ -361,8 +361,6 @@
 
 def full_rows(groups, blocks, columns, branch):
     panel, _, slots = blocks.shape[:3]
-    cols = columns[:, 0]
-    tile = place(blocks, cols)
     size = panel * BS
     sems = pltpu.SemaphoreType.DMA
     vmem = pl.BlockSpec(memory_space=pltpu.VMEM)
@@ -370,12 +368,15 @@
     updated, traces = pl.pallas_call(
         functools.partial(square_kernel, groups),
         out_shape=(
-            jax.ShapeDtypeStruct(blocks.shape, jnp.float32),
+            pltpu.VMEM(blocks.shape, jnp.float32),
             jax.ShapeDtypeStruct((8, BS), jnp.float32),
         ),
-        in_specs=[smem, smem, vmem, vmem],
+        in_specs=[smem, smem, pl.BlockSpec(memory_space=pl.ANY)],
         out_specs=(vmem, vmem),
         scratch_shapes=[
+            pltpu.VMEM((panel, slots, BS, BS), jnp.float32),
+            pltpu.VMEM((size, size), jnp.float32),
+            sems((panel,)),
             pltpu.VMEM((groups, size, size), jnp.float32),
             pltpu.VMEM((groups, size, size), jnp.float32),
             pltpu.VMEM((groups, size, size), jnp.bfloat16),
@@ -396,7 +397,7 @@
         compiler_params=pltpu.CompilerParams(
             collective_id=0, has_side_effects=True, vmem_limit_bytes=60 * 2**20
         ),
-    )(cols, branch, tile, blocks)
+    )(columns, branch, blocks)
     return updated, traces[0, :2]
 
 

time: 108 us -> 97.4 us (0.902)
  Pallas kernels: 101 us -> 94 us
  local copies, waits for them, and re-layouts: 5.78 us -> 2.59 us
    pallas_call x2 -> x1, Pallas kernels: 101 us -> 94 us  [full_rows(): pl.pallas_call(functools.partial(square_kernel, groups), out_shape=(pltpu...]
    unnamed x2 -> x1, local copies, waits for them, and re-layouts: 4.59 us -> 1.41 us
where the time goes in v2:
time: 97.4 us; the launch traced here: 97.2 us
  Pallas kernels  94 us (97%)
  local copies, waits for them, and re-layouts  2.59 us (3%)
    pallas_call x1, Pallas kernels, full_rows(): pl.pallas_call(functools.partial(square_kernel, groups), out_shape=(pltpu...  94 us

profile of v2, /device:TPU:0, one launch (start us, length us, event | category | flops | bytes accessed | tf_op | source)
XLA Modules:
  0.0 97.2 jit_solution(2087865724732850681)
XLA Ops:
  0.6 94.0 %shard_map.50 = (f32[6,1,6,128,128]{4,3,2,1,0:T(8,128)S(1)}, f32[8,128]{1,0:T(8,128)}) custom-call(s32[6,1,6]{2,1,0:T(1,128)} %cols_ref.1, s32[6]{0:T(128)} %branch_ref.1, f32[6,1,6,128,128]{4,3,2,1,0:T(8,128)} %blocks_hbm.1), custom_call_target="tpu_custom_call" | custom-call | tf_op jit(solution)/shard_map/pallas_call | solution.py:368
  94.6 1.4 %copy.6 = f32[6,1,6,128,128]{4,3,2,1,0:T(8,128)} copy(f32[6,1,6,128,128]{4,3,2,1,0:T(8,128)S(1)} %get-tuple-element.6) | data formatting | bytes 4718592
  96.0 1.2 %slice_bitcast_fusion = f32[2]{0:T(128)} fusion(f32[8,128]{1,0:T(8,128)} %get-tuple-element.5), kind=kLoop, calls=%fused_computation | loop fusion | bytes 16 | tf_op jit(solution)/shard_map/squeeze | solution.py:401

commit v3 on v2

--- a/solution.py
+++ b/solution.py
@@ -101,7 +101,7 @@
 
 def square_kernel(
     groups, cols_ref, branch_ref, blocks_hbm, out_ref, trace_ref,
-    blocks_ref, tile, in_sem, left, right, right_hi, right_lo, total, parts,
+    blocks_ref, tile, in_sem, left, right, right_hi, right_lo, total, turned, diagonal, parts,
     z_send, z_recv, p_send, p_recv, sz_send, sz_recv, sp_send, sp_recv, t_send, t_recv,
 ):
     row, col, depth = lax.axis_index("row"), lax.axis_index("col"), lax.axis_index("depth")
@@ -243,6 +243,21 @@
         for block in range(slots):
             piece = product[:, block * BS:(block + 1) * BS]
             total[block, at] = piece if first else total[block, at] + piece
+
+        @pl.when(row == col)
+        def _():
+            few = 32
+
+            def some(part, carry):
+                far = pl.ds(pl.multiple_of(at.start + part * few, few), few)
+                terms = source[far] * turned[index, far]
+                line = terms[:, :BS]
+                for block in range(1, slots):
+                    line = line + terms[:, block * BS:(block + 1) * BS]
+                diagonal[far] = line if first else diagonal[far] + line
+                return carry
+
+            lax.fori_loop(0, at.size // few, some, 0)
 
     def multiply_all(source, index, first=False):
         def some(part, carry):
@@ -269,6 +284,21 @@
     for axis in range(2):
         p_share(axis, CHUNKS, 1 - depth).wait_recv()
     split_right(right.at[corner], corner)
+
+    @pl.when(row == col)
+    def _():
+        def turn(source, index):
+            def some(block, carry):
+                at = pl.ds(pl.multiple_of(block * BS, BS), BS)
+                for other in range(slots):
+                    turned[index, at, other * BS:(other + 1) * BS] = source[other * BS:(other + 1) * BS, at].T
+                return carry
+            lax.fori_loop(0, panel, some, 0)
+
+        turn(tile, row)
+        for index in (across[0], across[1], corner):
+            turn(right.at[index], index)
+
     multiply_all(tile, col, True)
 
     def z_multiply(hop, chunk):
@@ -297,11 +327,10 @@
         new_sum = jnp.zeros((BS, BS), jnp.float32)
         for block in range(panel):
             at = pl.ds(block * BS, BS)
-            old = tile[at, at]
-            square = total[block, at]
-            new = jnp.where(branch_ref[block] == 1, square, 2.0 * old - square)
-            old_sum += jnp.where(eye, old, 0.0)
-            new_sum += jnp.where(eye, new, 0.0)
+            old = jnp.where(eye, tile[at, at], 0.0)
+            square = diagonal[at]
+            old_sum += old
+            new_sum += jnp.where(branch_ref[block] == 1, square, 2.0 * old - square)
         old_all, new_all = jnp.sum(old_sum), jnp.sum(new_sum)
         parts[row] = jnp.where(spot == 0, old_all, jnp.where(spot == 1, new_all, 0.0))
 
@@ -382,6 +411,8 @@
             pltpu.VMEM((groups, size, size), jnp.bfloat16),
             pltpu.VMEM((groups, size, size), jnp.bfloat16),
             pltpu.VMEM((slots, size, BS), jnp.float32),
+            pltpu.VMEM((groups, size, size), jnp.float32),
+            pltpu.VMEM((size, BS), jnp.float32),
             pltpu.VMEM((groups, 8, BS), jnp.float32),
             sems((2, groups - 1, CHUNKS)),
             sems((2, groups - 1, CHUNKS)),

time: 97.4 us -> 97.7 us (level)
  no operation moved by 1% of the time
where the time goes in v3:
time: 97.7 us; the launch traced here: 97.4 us
  Pallas kernels  94.2 us (96%)
  local copies, waits for them, and re-layouts  2.59 us (3%)
    pallas_call x1, Pallas kernels, full_rows(): pl.pallas_call(functools.partial(square_kernel, groups), out_shape=(pltpu...  94.2 us

profile of v3, /device:TPU:0, one launch (start us, length us, event | category | flops | bytes accessed | tf_op | source)
XLA Modules:
  0.0 97.4 jit_solution(12645904679554790858)
XLA Ops:
  0.6 94.2 %shard_map.50 = (f32[6,1,6,128,128]{4,3,2,1,0:T(8,128)S(1)}, f32[8,128]{1,0:T(8,128)}) custom-call(s32[6,1,6]{2,1,0:T(1,128)} %cols_ref.1, s32[6]{0:T(128)} %branch_ref.1, f32[6,1,6,128,128]{4,3,2,1,0:T(8,128)} %blocks_hbm.1), custom_call_target="tpu_custom_call" | custom-call | tf_op jit(solution)/shard_map/pallas_call | solution.py:397
  94.8 1.4 %copy.6 = f32[6,1,6,128,128]{4,3,2,1,0:T(8,128)} copy(f32[6,1,6,128,128]{4,3,2,1,0:T(8,128)S(1)} %get-tuple-element.6) | data formatting | bytes 4718592
  96.2 1.2 %slice_bitcast_fusion = f32[2]{0:T(128)} fusion(f32[8,128]{1,0:T(8,128)} %get-tuple-element.5), kind=kLoop, calls=%fused_computation | loop fusion | bytes 16 | tf_op jit(solution)/shard_map/squeeze | solution.py:432
